TPU v7x, 32 devices: a whole 2x2x4 slice. The times are simulated.
32 devices in a mesh: space: 8 (over y, x, core), level: 4 (over z).
Axes of the slice: x: 2, y: 2, z: 4, core: 2. Of those that a mesh axis runs over, the one named last changes fastest.
Arguments:
- fields: bfloat16 [4, 4096, 768], P('level', 'space'), may hold values from -16 to 16
- norm_vert: float32 [768], replicated, may hold values from 0.1 to 1.9
- query_vert: bfloat16 [768, 768], replicated, may hold values from -0.21875 to 0.21875
- keys_vert: bfloat16 [768, 768], replicated, may hold values from -0.21875 to 0.21875
- values_vert: bfloat16 [768, 768], replicated, may hold values from -0.21875 to 0.21875
- out_vert: bfloat16 [768, 768], replicated, may hold values from -0.21875 to 0.21875
- level_bias: float32 [12, 4, 4], replicated, may hold values from -3 to 250
- norm_patch: float32 [768], replicated, may hold values from 0.1 to 1.9
- query_patch: bfloat16 [768, 768], replicated, may hold values from -0.21875 to 0.21875
- keys_patch: bfloat16 [768, 768], replicated, may hold values from -0.21875 to 0.21875
- values_patch: bfloat16 [768, 768], replicated, may hold values from -0.21875 to 0.21875
- out_patch: bfloat16 [768, 768], replicated, may hold values from -0.21875 to 0.21875
- patch_bias: float32 [12, 2], replicated, may hold values from -3 to 250
- neighbours: int32 [16, 4], P('space'), may hold values from -1 to 15, as said below
- counts: int32 [16], P('space'), may hold values from 2 to 4, as said below
- cotangent: bfloat16 [4, 4096, 768], P('level', 'space'), may hold values from -0.046875 to 0.046875
Outputs:
- out_fields: bfloat16 [4, 4096, 768], P('level', 'space')
- grad_wo: float32 [768, 768], P('space')
Inputs may be any that keep to these rules, and one draw needn't show every extreme that they name: `neighbours`: row p lists distinct patches, at most one from each device of space, held on devices at cycle distance 1 to 2 from the device of patch p (device s of space holds patches s * 2 to (s + 1) * 2 - 1); entries from counts[p] on are -1. `counts`: some patch has 4 neighbours in every draw.
All inputs are finite; a program needn't handle non-finite values.
Results may differ from a plain program's by a relative error of at most 0.025.
Values may be sent and summed in bfloat16 or wider, within the bound.
A program may use at most 128 MiB of HBM per device.

v0:
```python
import functools
import math

import jax
import jax.numpy as jnp
from jax import lax
from jax.experimental import pallas as pl
from jax.experimental.pallas import tpu as pltpu
from jax.sharding import PartitionSpec as P

HD = 64
PATCH = 256
LANES = 128
SPLIT = 2
VMEM_LIMIT = 58 * 1024 * 1024

epsilon = 1e-06


def normalized(widened, scaling):
    mean_square = jnp.mean(widened * widened, axis=-1, keepdims=True)
    return (widened * lax.rsqrt(mean_square + epsilon) * scaling).astype(jnp.bfloat16)


def project(inputs, weight):
    return jnp.dot(inputs, weight, preferred_element_type=jnp.float32).astype(jnp.bfloat16)


def vertical(x, gain, wq, wk, wv, wo, bias_rows, attn_ref):
    levels, columns, features = x.shape
    tokens = levels * columns
    x = x.reshape(tokens, features).astype(jnp.float32)
    normed = normalized(x, gain)
    queries = project(normed, wq).astype(jnp.float32)
    keys = project(normed, wk).astype(jnp.float32)
    values = project(normed, wv).astype(jnp.float32)
    head_of = lax.broadcasted_iota(jnp.int32, (features, LANES), 0) // HD
    gather_heads = (head_of == lax.broadcasted_iota(jnp.int32, (features, LANES), 1)).astype(jnp.bfloat16)
    head_to = lax.broadcasted_iota(jnp.int32, (LANES, features), 1) // HD
    spread_heads = (head_to == lax.broadcasted_iota(jnp.int32, (LANES, features), 0)).astype(jnp.bfloat16)
    for i in range(levels):
        query = queries[i * columns : (i + 1) * columns]
        products = jnp.concatenate(
            [(query * keys[j * columns : (j + 1) * columns]).astype(jnp.bfloat16) for j in range(levels)], axis=0
        )
        summed = jnp.dot(products, gather_heads, preferred_element_type=jnp.float32) * HD ** (-0.5)
        scores = [
            summed[j * columns : (j + 1) * columns] + bias_rows[i * levels + j]
            for j in range(levels)
        ]
        top = functools.reduce(jnp.maximum, scores)
        raised = [jnp.exp(score - top) for score in scores]
        inverse = 1.0 / functools.reduce(jnp.add, raised)
        weights = jnp.concatenate([(each * inverse).astype(jnp.bfloat16) for each in raised], axis=0)
        spread = jnp.dot(weights, spread_heads, preferred_element_type=jnp.float32)
        mixed = functools.reduce(
            jnp.add,
            [
                spread[j * columns : (j + 1) * columns] * values[j * columns : (j + 1) * columns]
                for j in range(levels)
            ],
        )
        attn_ref[i * columns : (i + 1) * columns, :] = mixed.astype(jnp.bfloat16)
    hidden = x + jnp.dot(attn_ref[...], wo, preferred_element_type=jnp.float32)
    return hidden.astype(jnp.bfloat16).reshape(levels, columns, features)


def choices(nb_ref, count_ref, patch, source, per_device):
    live = jnp.int32(0)
    within = jnp.int32(0)
    for m in range(nb_ref.shape[1]):
        listed = jnp.maximum(nb_ref[patch, m], 0)
        hit = jnp.logical_and(m < count_ref[patch], lax.div(listed, per_device) == source)
        live = jnp.where(hit, 1, live)
        within = jnp.where(hit, lax.rem(listed, per_device), within)
    return live, within


def attend(step, q_ref, k_ref, v_ref, attn_ref, pb_ref, tables, far, slots, early, top_ref, total_ref, mixed_ref):
    low = lax.broadcasted_iota(jnp.int32, (1, LANES), 1) < HD
    lanes = pl.ds(pl.multiple_of(step * LANES, LANES), LANES)
    for patch, picked in enumerate(tables):
        rows = pl.ds(patch * PATCH, PATCH)
        blocks = [slot * len(tables) + picked[slot][1] for slot in slots]
        if early:
            blocks = [far + patch] + blocks
        query = q_ref[rows, lanes]
        results = []
        for parity in range(2):
            head = step * 2 + parity
            mine = low if parity == 0 else jnp.logical_not(low)
            masked = jnp.where(mine, query, jnp.zeros_like(query))
            scores = [
                lax.dot_general(
                    masked, k_ref[block, :, lanes], (((1,), (1,)), ((), ())), preferred_element_type=jnp.float32
                )
                for block in blocks
            ]
            adds = [jnp.where(picked[slot][0] > 0, pb_ref[1, head], jnp.float32(-1e30)) for slot in slots]
            if early:
                adds = [pb_ref[0, head]] + adds
            top = functools.reduce(
                jnp.maximum, [jnp.max(s, axis=-1, keepdims=True) + a for s, a in zip(scores, adds)]
            )
            if not early:
                before = top_ref[rows, lanes][:, parity * HD : parity * HD + 1]
                top = jnp.maximum(top, before)
            raised = [jnp.exp(s + (a - top)) for s, a in zip(scores, adds)]
            total = functools.reduce(jnp.add, [jnp.sum(r, axis=-1, keepdims=True) for r in raised])
            mixed = functools.reduce(
                jnp.add,
                [
                    jnp.dot(r.astype(jnp.bfloat16), v_ref[block, :, lanes], preferred_element_type=jnp.float32)
                    for r, block in zip(raised, blocks)
                ],
            )
            if early:
                results.append((top, total, mixed))
            else:
                fade = jnp.exp(before - top)
                total = total + total_ref[rows, lanes][:, parity * HD : parity * HD + 1] * fade
                results.append((mixed + mixed_ref[rows, lanes] * fade) / total)
        if early:
            for ref, even, odd in zip((top_ref, total_ref, mixed_ref), *results):
                ref[rows, lanes] = jnp.where(low, even, odd)
        else:
            attn_ref[rows, lanes] = jnp.where(low, results[0], results[1]).astype(jnp.bfloat16)


def remote(src, dst, send, recv, device):
    return pltpu.make_async_remote_copy(
        src_ref=src, dst_ref=dst, send_sem=send, recv_sem=recv, device_id=device,
        device_id_type=pl.DeviceIdType.MESH,
    )


def whole_kernel(cycle, levels, x_ref, nv_ref, np_ref, wqv_hbm, wkv_hbm, wvv_hbm, wov_hbm, wqp_hbm, wkp_hbm, wvp_hbm,
                 wop_hbm, cot_hbm, lb_ref, pb_ref, nb_ref, count_ref, out_ref, grad_ref, weight_ref, cot_ref, in_ref,
                 hsend_ref, hid_ref, attn_ref, own_ref, far_ref, q_ref, k_ref, v_ref, gsend_ref, grecv_ref, lsend_ref,
                 lrecv_ref, final_ref, top_ref, total_ref, mixed_ref, load_sem, in_send, in_recv, back_send, back_recv, halo_send, halo_recv,
                 share_send, share_recv, part_send, part_recv, full_send, full_recv):
    chunks, _, columns, features = x_ref.shape
    place = lax.axis_index("space")
    level = lax.axis_index("level")
    weights_hbm = (wqv_hbm, wkv_hbm, wvv_hbm, wov_hbm, wqp_hbm, wkp_hbm, wvp_hbm, wop_hbm)
    loads = [pltpu.make_async_copy(w, weight_ref.at[i], load_sem.at[i]) for i, w in enumerate(weights_hbm)]
    loads.append(pltpu.make_async_copy(cot_hbm, cot_ref, load_sem.at[len(weights_hbm)]))
    for load in loads:
        load.start()

    barrier = pltpu.get_barrier_semaphore()
    peers = [lax.rem(level + k, levels) for k in range(1, levels)]
    around = [lax.rem(place + k, cycle) for k in range(1, cycle)]
    for peer in peers:
        pl.semaphore_signal(barrier, inc=1, device_id={"level": peer}, device_id_type=pl.DeviceIdType.MESH)
    for peer in around:
        pl.semaphore_signal(barrier, inc=1, device_id={"space": peer}, device_id_type=pl.DeviceIdType.MESH)
    pl.semaphore_wait(barrier, levels - 1 + cycle - 1)

    inward, back, halo = [], [], []

    def send_in(c):
        steps = []
        for k, peer in enumerate(peers):
            steps.append(remote(x_ref.at[c, peer], in_ref.at[c, level], in_send.at[c, k], in_recv.at[c, k],
                                {"level": peer}))
            steps[-1].start()
        in_ref[c, level] = x_ref[c, level]
        inward.append(steps)

    for c in range(min(2, chunks)):
        send_in(c)

    lane = lax.broadcasted_iota(jnp.int32, (1, LANES), 1)
    bias_rows = []
    for i in range(levels):
        for j in range(levels):
            row = jnp.zeros((1, LANES), jnp.float32)
            for h in range(lb_ref.shape[2]):
                row = jnp.where(lane == h, lb_ref[i, j, h], row)
            bias_rows.append(row)
    for load in loads[:4]:
        load.wait()

    def vertical_step(c):
        for step in inward[c]:
            step.wait_recv()
        hsend_ref[c] = vertical(in_ref[c], nv_ref[...][None], weight_ref[0], weight_ref[1], weight_ref[2],
                                weight_ref[3], bias_rows, attn_ref.at[pl.ds(0, levels * columns)])
        steps = []
        for k, peer in enumerate(peers):
            steps.append(remote(hsend_ref.at[c, peer], hid_ref.at[c, level], back_send.at[c, k], back_recv.at[c, k],
                                {"level": peer}))
            steps[-1].start()
        hid_ref[c, level] = hsend_ref[c, level]
        back.append(steps)
        if c + 2 < chunks:
            send_in(c + 2)

    toward = lax.rem(place, 2) * 2 - 1
    sources = [lax.rem(place + step * toward + 2 * cycle, cycle) for step in (1, 2, -1, -2)]
    partner = sources[2]
    patches = chunks // SPLIT
    far = len(sources) * patches
    scale = jnp.bfloat16(HD ** (-0.5))

    def halo_step(c):
        for step in back[c]:
            step.wait_recv()
        own_ref[c] = normalized(
            hid_ref[c].reshape(levels * columns, features).astype(jnp.float32), np_ref[...][None]
        )
        steps = []
        for slot, target in ((0, sources[0]), (1, sources[3]), (2, partner)):
            steps.append(remote(own_ref.at[c], far_ref.at[slot * chunks + c], halo_send.at[c, slot],
                                halo_recv.at[c, slot], {"space": target}))
            steps[-1].start()
        halo.append(steps)

    def own_step(patch):
        normed = own_ref[patch * SPLIT : (patch + 1) * SPLIT].reshape(PATCH, features)
        q_ref[pl.ds(patch * PATCH, PATCH), :] = project(normed, weight_ref[4]) * scale
        k_ref[far + patch] = project(normed, weight_ref[5])
        v_ref[far + patch] = project(normed, weight_ref[6])

    def forward(c):
        halo[c][0].wait_recv()
        passed = remote(far_ref.at[c], far_ref.at[3 * chunks + c], halo_send.at[c, 3], halo_recv.at[c, 3],
                        {"space": partner})
        passed.start()
        halo[c].append(passed)

    def distant(slot, patch):
        if slot:
            for c in range(patch * SPLIT, (patch + 1) * SPLIT):
                halo[c][slot].wait_recv()
        start = slot * chunks + patch * SPLIT
        block = far_ref[start : start + SPLIT].reshape(PATCH, features)
        k_ref[slot * patches + patch] = project(block, weight_ref[5])
        v_ref[slot * patches + patch] = project(block, weight_ref[6])

    loaded = False
    for c in range(chunks):
        vertical_step(c)
        if c >= 1:
            halo_step(c - 1)
        if not loaded:
            for load in loads[4:]:
                load.wait()
            loaded = True
    for patch in range(patches - 1):
        own_step(patch)
        distant(2, patch)
    halo_step(chunks - 1)
    for c in range(chunks - SPLIT):
        forward(c)
    own_step(patches - 1)
    distant(2, patches - 1)
    for patch in range(patches - 1):
        for slot in (0, 1, 3):
            distant(slot, patch)
    pairs = features // LANES
    tables = [[choices(nb_ref, count_ref, patch, source, patches) for source in sources] for patch in range(patches)]
    states = (top_ref, total_ref, mixed_ref)

    def early_pair(step, carry):
        attend(step, q_ref, k_ref, v_ref, attn_ref, pb_ref, tables, far, (2,), True, *states)
        return carry

    for c in range(chunks - SPLIT, chunks - 1):
        forward(c)
    lax.fori_loop(0, pairs, early_pair, 0)
    forward(chunks - 1)
    for slot in (0, 1, 3):
        distant(slot, patches - 1)

    share = features // cycle
    grain = gsend_ref.shape[1]
    per_pair = LANES // grain
    per_owner = share // grain

    def share_of(index):
        owner = index // per_owner
        part = lax.rem(index, per_owner)
        gap = lax.rem(place - owner + cycle, cycle)
        slot = jnp.maximum(gap - 1, 0) * per_owner + part
        return owner, remote(gsend_ref.at[index], grecv_ref.at[slot], share_send.at[index], share_recv.at[slot],
                             {"space": owner})

    def pair(turn, carry):
        step = lax.rem(place * pairs // cycle + 1 + turn, pairs)
        attend(step, q_ref, k_ref, v_ref, attn_ref, pb_ref, tables, far, (0, 1, 3), False, *states)
        lanes = pl.ds(pl.multiple_of(step * LANES, LANES), LANES)
        total = lax.dot_general(
            attn_ref[:, lanes], cot_ref[...], (((0,), (0,)), ((), ())), preferred_element_type=jnp.float32
        ).astype(jnp.bfloat16)
        for part in range(per_pair):
            gsend_ref[step * per_pair + part] = total[part * grain : (part + 1) * grain]
        for part in range(per_pair):
            owner, copy = share_of(step * per_pair + part)

            @pl.when(owner != place)
            def _():
                copy.start()

        return carry

    lax.fori_loop(0, pairs, pair, 0)
    out_ref[...] = (
        hid_ref[...].reshape(patches * PATCH, features).astype(jnp.float32)
        + jnp.dot(attn_ref[...], weight_ref[7], preferred_element_type=jnp.float32)
    ).astype(jnp.bfloat16)
    sums = []
    for part in range(per_owner):
        sums.append(gsend_ref[place * per_owner + part].astype(jnp.float32))
        for k in range(cycle - 1):
            slot = k * per_owner + part
            remote(gsend_ref.at[0], grecv_ref.at[slot], share_send.at[0], share_recv.at[slot],
                   {"space": partner}).wait_recv()
            sums[-1] = sums[-1] + grecv_ref[slot].astype(jnp.float32)
    gathered = jnp.concatenate(sums, axis=0)
    piece = share // levels
    for i in range(levels):
        lsend_ref[i] = gathered[i * piece : (i + 1) * piece].astype(jnp.bfloat16)
    parts = []
    for k, peer in enumerate(peers):
        parts.append(remote(lsend_ref.at[peer], lrecv_ref.at[k], part_send.at[k], part_recv.at[k], {"level": peer}))
        parts[-1].start()
    gathered = lsend_ref[level].astype(jnp.float32)
    for k, step in enumerate(parts):
        step.wait_recv()
        gathered = gathered + lrecv_ref[k].astype(jnp.float32)
    final_ref[level] = gathered.astype(jnp.bfloat16)
    fulls = []
    for k, peer in enumerate(peers):
        fulls.append(remote(final_ref.at[level], final_ref.at[level], full_send.at[k], full_recv.at[k],
                            {"level": peer}))
        fulls[-1].start()
    for step in fulls:
        step.wait_recv()
    for i in range(levels):
        grad_ref[i * piece : (i + 1) * piece, :] = final_ref[i].astype(jnp.float32)
    for steps in inward + back + halo + [parts, fulls]:
        for step in steps:
            step.wait_send()

    def drained(index, carry):
        owner, copy = share_of(index)

        @pl.when(owner != place)
        def _():
            copy.wait_send()

        return carry

    lax.fori_loop(0, pairs * per_pair, drained, 0)


def body(fields, norm_vert, query_vert, keys_vert, values_vert, out_vert, level_bias, norm_patch, query_patch,
         keys_patch, values_patch, out_patch, patch_bias, neighbours, counts, cotangent):
    _, tokens, features = fields.shape
    levels = lax.axis_size("level")
    cycle = lax.axis_size("space")
    patches = tokens // PATCH
    chunks = patches * SPLIT
    columns = PATCH // SPLIT // levels
    grain = math.gcd(features // cycle, LANES)
    share = features // cycle
    x = fields.reshape(chunks, levels, columns, features)
    vmem = pl.BlockSpec(memory_space=pltpu.VMEM)
    smem = pl.BlockSpec(memory_space=pltpu.SMEM)
    hbm = pl.BlockSpec(memory_space=pl.ANY)
    narrow = lambda *shape: pltpu.VMEM(shape, jnp.bfloat16)
    dma = lambda *shape: pltpu.SemaphoreType.DMA(shape)
    blocks = 5 * patches
    out, grad = pl.pallas_call(
        functools.partial(whole_kernel, cycle, levels),
        out_shape=(
            jax.ShapeDtypeStruct((tokens, features), jnp.bfloat16),
            jax.ShapeDtypeStruct((share, features), jnp.float32),
        ),
        in_specs=[vmem] * 3 + [hbm] * 9 + [smem] * 4,
        out_specs=(vmem, vmem),
        scratch_shapes=[
            narrow(8, features, features),
            narrow(tokens, features),
            narrow(chunks, levels, columns, features),
            narrow(chunks, levels, columns, features),
            narrow(chunks, levels, columns, features),
            narrow(tokens, features),
            narrow(chunks, PATCH // SPLIT, features),
            narrow(4 * chunks, PATCH // SPLIT, features),
            narrow(tokens, features),
            narrow(blocks, PATCH, features),
            narrow(blocks, PATCH, features),
            narrow(features // grain, grain, features),
            narrow((cycle - 1) * share // grain, grain, features),
            narrow(levels, share // levels, features),
            narrow(levels - 1, share // levels, features),
            narrow(levels, share // levels, features),
            pltpu.VMEM((tokens, features), jnp.float32),
            pltpu.VMEM((tokens, features), jnp.float32),
            pltpu.VMEM((tokens, features), jnp.float32),
            dma(9),
            dma(chunks, levels - 1),
            dma(chunks, levels - 1),
            dma(chunks, levels - 1),
            dma(chunks, levels - 1),
            dma(chunks, 4),
            dma(chunks, 4),
            dma(features // grain),
            dma((cycle - 1) * share // grain),
            dma(levels - 1),
            dma(levels - 1),
            dma(levels - 1),
            dma(levels - 1),
        ],
        compiler_params=pltpu.CompilerParams(
            collective_id=0, has_side_effects=True, vmem_limit_bytes=VMEM_LIMIT
        ),
        name="whole_block",
    )(x, norm_vert, norm_patch, query_vert, keys_vert, values_vert, out_vert, query_patch, keys_patch,
      values_patch, out_patch, cotangent[0], jnp.transpose(level_bias, (1, 2, 0)), patch_bias.T, neighbours, counts)
    return (out[None], grad)


def solution(mesh):
    split = P("level", "space", None)
    return jax.shard_map(
        body,
        mesh=mesh,
        in_specs=(split,) + (P(),) * 12 + (P("space", None), P("space"), split),
        out_specs=(split, P("space", None)),
        check_vma=False,
    )
```

profile of v0, /device:TPU:0, one launch (start us, length us, event | category | flops | bytes accessed | tf_op | source)
XLA Modules:
  0.0 94.6 jit_solution(14524133215864026340)
XLA Ops:
  0.6 91.2 %whole_block.1 = (bf16[512,768]{1,0:T(8,128)(2,1)}, f32[96,768]{1,0:T(8,128)}) custom-call(bf16[4,4,32,768]{3,2,1,0:T(8,128)(2,1)} %bitcast.5, f32[768]{0:T(1024)} %nv_ref.1, f32[768]{0:T(1024)} %np_ref.1, bf16[768,768]{1,0:T(8,128)(2,1)} %wqv_hbm.1, bf16[768,768]{1,0:T(8,128)(2,1)} %wkv_hbm.1, bf16[768,768]{1,0:T(8,128)(2,1)} %wvv_hbm.1, ...), custom_call_target="tpu_custom_call" | custom-call | tf_op jit(solution)/shard_map/whole_block/pallas_call | solution.py:376
  91.8 0.0 copy-start
  91.8 2.1 %copy.20 = bf16[1,512,768]{2,1,0:T(8,128)(2,1)} copy(bf16[1,512,768]{2,1,0:T(8,128)(2,1)} %bitcast.7) | data formatting | bytes 1572864
  93.9 0.0 copy-done
  93.9 0.7 copy.21
Async XLA Ops:
  91.8 2.1 %copy-start = (f32[96,768]{1,0:T(8,128)S(1)}, f32[96,768]{1,0:T(8,128)}, u32[]{:S(2)}) copy-start(f32[96,768]{1,0:T(8,128)} %get-tuple-element.9) | copy-start | bytes 884740
where the time goes:
time: 94.8 us; the launch traced here: 94.6 us
  Pallas kernels  91.2 us (96%)
  local copies, waits for them, and re-layouts  2.83 us (3%)
    pallas_call x1, Pallas kernels, body(): pl.pallas_call(functools.partial(whole_kernel, cycle, levels), out_shape=...  91.2 us
    unnamed x4, local copies, waits for them, and re-layouts  2.83 us

commit v1 on v0

v1 whole, which is shorter than its diff:
```python
import functools
import math

import jax
import jax.numpy as jnp
from jax import lax
from jax.experimental import pallas as pl
from jax.experimental.pallas import tpu as pltpu
from jax.sharding import PartitionSpec as P

HD = 64
PATCH = 256
LANES = 128
ROWS = 16
DEPTH = 3
VMEM_LIMIT = 58 * 1024 * 1024

epsilon = 1e-06


def normalized(widened, scaling):
    mean_square = jnp.mean(widened * widened, axis=-1, keepdims=True)
    return (widened * lax.rsqrt(mean_square + epsilon) * scaling).astype(jnp.bfloat16)


def project(inputs, weight):
    return jnp.dot(inputs, weight, preferred_element_type=jnp.float32).astype(jnp.bfloat16)


def vertical(x, gain, wq, wk, wv, wo, bias_rows, gather_heads, spread_heads):
    levels, columns, features = x.shape
    tokens = levels * columns
    x = x.reshape(tokens, features).astype(jnp.float32)
    normed = normalized(x, gain)
    queries = project(normed, wq).astype(jnp.float32)
    keys = project(normed, wk).astype(jnp.float32)
    values = project(normed, wv).astype(jnp.float32)
    part = lambda array, i: array[i * columns : (i + 1) * columns]
    products = jnp.concatenate(
        [(part(queries, i) * part(keys, j)).astype(jnp.bfloat16) for i in range(levels) for j in range(levels)], axis=0
    )
    summed = jnp.dot(products, gather_heads, preferred_element_type=jnp.float32) * HD ** (-0.5)
    weights = []
    for i in range(levels):
        scores = [part(summed, i * levels + j) + bias_rows[i * levels + j] for j in range(levels)]
        top = functools.reduce(jnp.maximum, scores)
        raised = [jnp.exp(score - top) for score in scores]
        inverse = 1.0 / functools.reduce(jnp.add, raised)
        weights += [(each * inverse).astype(jnp.bfloat16) for each in raised]
    spread = jnp.dot(jnp.concatenate(weights, axis=0), spread_heads, preferred_element_type=jnp.float32)
    mixed = [
        functools.reduce(jnp.add, [part(spread, i * levels + j) * part(values, j) for j in range(levels)])
        for i in range(levels)
    ]
    attn = jnp.concatenate(mixed, axis=0).astype(jnp.bfloat16)
    hidden = x + jnp.dot(attn, wo, preferred_element_type=jnp.float32)
    return hidden.astype(jnp.bfloat16).reshape(levels, columns, features)


def choices(nb_ref, count_ref, patch, source, per_device):
    live = jnp.int32(0)
    within = jnp.int32(0)
    for m in range(nb_ref.shape[1]):
        listed = jnp.maximum(nb_ref[patch, m], 0)
        hit = jnp.logical_and(m < count_ref[patch], lax.div(listed, per_device) == source)
        live = jnp.where(hit, 1, live)
        within = jnp.where(hit, lax.rem(listed, per_device), within)
    return live, within


def score(step, patch, parity, parts, q_ref, k_ref):
    low = lax.broadcasted_iota(jnp.int32, (1, LANES), 1) < HD
    mine = low if parity == 0 else jnp.logical_not(low)
    lanes = pl.ds(pl.multiple_of(step * LANES, LANES), LANES)
    query = q_ref[pl.ds(patch * PATCH, PATCH), lanes]
    query = jnp.where(mine, query, jnp.zeros_like(query))
    keys = jnp.concatenate([k_ref[block, pl.ds(first, count), lanes] for block, first, count, _ in parts], axis=0)
    return lax.dot_general(keys, query, (((1,), (1,)), ((), ())), preferred_element_type=jnp.float32)


def soften(scores, parts, before):
    pieces, at = [], 0
    for _, _, count, add in parts:
        pieces.append((scores[at : at + count], add))
        at += count
    top = functools.reduce(jnp.maximum, [jnp.max(s, axis=0, keepdims=True) + a for s, a in pieces])
    if before is not None:
        top = jnp.maximum(top, before)
    raised = [jnp.exp2(s + (a - top)) for s, a in pieces]
    total = functools.reduce(jnp.add, [jnp.sum(r, axis=0, keepdims=True) for r in raised])
    return top, total, jnp.concatenate([r.astype(jnp.bfloat16) for r in raised], axis=0)


def mix(step, parity, raised, parts, vt_ref):
    rows = pl.ds(pl.multiple_of(step * LANES + parity * HD, HD), HD)
    values = jnp.concatenate([vt_ref[block, rows, pl.ds(first, count)] for block, first, count, _ in parts], axis=1)
    return jnp.dot(values, raised, preferred_element_type=jnp.float32)


def attend(step, patches, second, parts_of, q_ref, k_ref, vt_ref, top_ref, finish):
    heads = [(patch, parity) for patch in range(patches) for parity in range(2)]
    parts = [parts_of(patch, step * 2 + parity, second) for patch, parity in heads]
    slots = [patch * top_ref.shape[0] // patches + step * 2 + parity for patch, parity in heads]
    befores = [top_ref[slot] if second else None for slot in slots]
    scores, soft = {}, {}
    for turn in range(len(heads) + 2):
        if turn < len(heads):
            patch, parity = heads[turn]
            scores[turn] = score(step, patch, parity, parts[turn], q_ref, k_ref)
        if 1 <= turn < len(heads) + 1:
            soft[turn - 1] = soften(scores.pop(turn - 1), parts[turn - 1], befores[turn - 1])
        if turn >= 2:
            at = turn - 2
            top, total, raised = soft.pop(at)
            finish(slots[at], *heads[at], befores[at], top, total, mix(step, heads[at][1], raised, parts[at], vt_ref))


def remote(src, dst, send, recv, device):
    return pltpu.make_async_remote_copy(
        src_ref=src, dst_ref=dst, send_sem=send, recv_sem=recv, device_id=device,
        device_id_type=pl.DeviceIdType.MESH,
    )


def whole_kernel(cycle, levels, x_ref, nv_ref, np_ref, wqv_hbm, wkv_hbm, wvv_hbm, wov_hbm, wqp_hbm, wkp_hbm, wvp_hbm,
                 wop_hbm, cot_hbm, lb_ref, pb_ref, nb_ref, count_ref, out_ref, grad_ref, weight_ref, wvt_ref, gather_ref,
                 spread_ref, cot_ref, in_ref, hsend_ref, hid_ref, own_ref, far_ref, q_ref, k_ref, vt_ref, attn_ref,
                 gsend_ref, gpair_ref, gsum_ref, grecv_ref, lsend_ref, lrecv_ref, final_ref, top_ref, total_ref, mixed_ref, load_sem, in_send,
                 in_recv, back_send, back_recv, halo_send, halo_recv, pair_send, pair_recv, share_send, share_recv, part_send, part_recv,
                 full_send, full_recv):
    chunks, _, columns, features = x_ref.shape
    size = levels * columns
    split = PATCH // size
    patches = chunks // split
    half = max(LANES, size)
    group = half // size
    order = [patch * split + turn for turn in range(split) for patch in range(patches)]
    place = lax.axis_index("space")
    level = lax.axis_index("level")
    weights_hbm = (wqv_hbm, wkv_hbm, wvv_hbm, wov_hbm, wqp_hbm, wkp_hbm, wvp_hbm, wop_hbm)
    loads = [pltpu.make_async_copy(w, weight_ref.at[i], load_sem.at[i]) for i, w in enumerate(weights_hbm)]
    loads.append(pltpu.make_async_copy(cot_hbm, cot_ref, load_sem.at[len(weights_hbm)]))
    for load in loads:
        load.start()

    barrier = pltpu.get_barrier_semaphore()
    peers = [lax.rem(level + k, levels) for k in range(1, levels)]
    around = [lax.rem(place + k, cycle) for k in range(1, cycle)]
    for peer in peers:
        pl.semaphore_signal(barrier, inc=1, device_id={"level": peer}, device_id_type=pl.DeviceIdType.MESH)
    for peer in around:
        pl.semaphore_signal(barrier, inc=1, device_id={"space": peer}, device_id_type=pl.DeviceIdType.MESH)
    pl.semaphore_wait(barrier, levels - 1 + cycle - 1)

    inward, back, sent = [], [], []

    def send_in(i):
        c = order[i]
        steps = []
        for k, peer in enumerate(peers):
            steps.append(remote(x_ref.at[c, peer], in_ref.at[c, level], in_send.at[c, k], in_recv.at[c, k],
                                {"level": peer}))
            steps[-1].start()
        in_ref[c, level] = x_ref[c, level]
        inward.append(steps)

    for i in range(min(DEPTH, chunks)):
        send_in(i)

    lane = lax.broadcasted_iota(jnp.int32, (1, LANES), 1)
    bias_rows = []
    for i in range(levels):
        for j in range(levels):
            row = jnp.zeros((1, LANES), jnp.float32)
            for h in range(lb_ref.shape[2]):
                row = jnp.where(lane == h, lb_ref[i, j, h], row)
            bias_rows.append(row)
    head_of = lax.broadcasted_iota(jnp.int32, (features, LANES), 0) // HD
    gather_ref[...] = (head_of == lax.broadcasted_iota(jnp.int32, (features, LANES), 1)).astype(jnp.bfloat16)
    head_to = lax.broadcasted_iota(jnp.int32, (LANES, features), 1) // HD
    spread_ref[...] = (head_to == lax.broadcasted_iota(jnp.int32, (LANES, features), 0)).astype(jnp.bfloat16)
    for load in loads[:4]:
        load.wait()

    def vertical_step(i):
        c = order[i]
        for step in inward[i]:
            step.wait_recv()
        hsend_ref[c] = vertical(in_ref[c], nv_ref[...][None], weight_ref[0], weight_ref[1], weight_ref[2],
                                weight_ref[3], bias_rows, gather_ref[...], spread_ref[...])
        steps = []
        for k, peer in enumerate(peers):
            steps.append(remote(hsend_ref.at[c, peer], hid_ref.at[c, level], back_send.at[c, k], back_recv.at[c, k],
                                {"level": peer}))
            steps[-1].start()
        hid_ref[c, level] = hsend_ref[c, level]
        back.append(steps)
        if i + DEPTH < chunks:
            send_in(i + DEPTH)
        if i == 0:
            for load in loads[4:]:
                load.wait()
            wvt_ref[...] = weight_ref[6].T

    chips = cycle // 2
    chip, core = lax.div(place, 2), lax.rem(place, 2)
    toward = core * 2 - 1
    sources = [lax.rem(place + step * toward + 2 * cycle, cycle) for step in (1, 2, -1, -2)]
    partner = sources[2]
    far = len(sources) * patches
    scale = HD ** (-0.5) * math.log2(math.e)
    relayed = chips == 4
    odd = lax.rem(chip + core, 2)
    near, diagonal = (3 - 2 * odd, 1 + 2 * odd) if relayed else (1, 3)
    beside = (chip + 1 - 2 * lax.rem(chip, 2)) * 2 + core
    across = lax.rem(chip + 2, chips) * 2 + core

    def halo_copy(c, src, slot, lane_of, device):
        return remote(src, far_ref.at[slot, c], halo_send.at[c, lane_of], halo_recv.at[c, slot], {"space": device})

    def begin(make):
        make().start()
        sent.append(make)

    def halo_step(i):
        c = order[i]
        for step in back[i]:
            step.wait_recv()
        own_ref[c] = normalized(hid_ref[c].reshape(size, features).astype(jnp.float32), np_ref[...][None])
        if relayed:
            begin(lambda: halo_copy(c, own_ref.at[c], diagonal, 0, beside))
        else:
            begin(lambda: halo_copy(c, own_ref.at[c], 3, 0, sources[1]))
            begin(lambda: halo_copy(c, own_ref.at[c], 1, 2, sources[3]))
        begin(lambda: halo_copy(c, own_ref.at[c], 2, 1, partner))

    def relay_step(i):
        c = order[i]
        halo_copy(c, own_ref.at[c], near, 0, beside).wait_recv()
        if relayed:
            begin(lambda: halo_copy(c, far_ref.at[near, c], diagonal, 2, across))

    def forward_step(i):
        c = order[i]
        halo_copy(c, own_ref.at[c], diagonal, 0, across).wait_recv()
        begin(lambda: halo_copy(c, far_ref.at[3, c], 0, 3, partner))

    def members(patch, part):
        return [patch * split + part * group + k for k in range(group)]

    def keys_values(normed, blocks, part):
        keys = project(normed, weight_ref[5])
        values = lax.dot_general(
            wvt_ref[...], normed, (((1,), (1,)), ((), ())), preferred_element_type=jnp.float32
        ).astype(jnp.bfloat16)
        for k, block in enumerate(blocks):
            k_ref[block, part * half : (part + 1) * half, :] = keys[k * half : (k + 1) * half]
            vt_ref[block, :, part * half : (part + 1) * half] = values[:, k * half : (k + 1) * half]

    def own_half(patch, part):
        first = members(patch, part)[0]
        normed = own_ref[first : first + group].reshape(half, features)
        queries = jnp.dot(normed, weight_ref[4], preferred_element_type=jnp.float32) * scale
        q_ref[first * size : first * size + half, :] = queries.astype(jnp.bfloat16)
        keys_values(normed, (far + patch,), part)

    def far_half(slots, patch, part):
        first = members(patch, part)[0]
        for slot in slots:
            if slot in (0, 2):
                for c in members(patch, part):
                    halo_copy(c, own_ref.at[c], slot, 1, partner).wait_recv()
        normed = jnp.concatenate([far_ref[slot, first : first + group].reshape(half, features) for slot in slots], axis=0)
        keys_values(normed, [slot * patches + patch for slot in slots], part)

    halves = PATCH // half
    arrival = [i + 2.4 if i < chunks - 2 else chunks - 0.6 + 0.5 * (i - chunks + 3) for i in range(chunks)]
    events = []
    for i in range(chunks):
        events.append((float(i), vertical_step, (i,)))
        events.append((arrival[i], halo_step, (i,)))
        events.append((arrival[i] + 0.9, relay_step, (i,)))
        events.append((arrival[i] + 1.8, forward_step, (i,)))
    for patch in range(patches):
        for part in range(halves):
            last = order.index(members(patch, part)[-1])
            events.append((arrival[last] + 0.05, own_half, (patch, part)))
            events.append((arrival[last] + 0.35, far_half, ((2,), patch, part)))
            events.append((arrival[last] + 2.2, far_half, ((1, 3, 0), patch, part)))
    events.sort(key=lambda event: event[0])
    start = arrival[-1] + 0.5
    pairs = features // LANES
    late = [event for event in events if event[0] > start]
    for _, act, args in events:
        if _ <= start:
            act(*args)
    tables = [[choices(nb_ref, count_ref, patch, source, patches) for source in sources] for patch in range(patches)]

    def parts_of(patch, head, second):
        log2e = jnp.float32(math.log2(math.e))
        adds = [jnp.where(live > 0, pb_ref[1, head], jnp.float32(-1e30)) * log2e for live, _ in tables[patch]]
        block = [slot * patches + tables[patch][slot][1] for slot in range(len(sources))]
        count = PATCH - half
        if second:
            return [(block[slot], count, half, adds[slot]) for slot in (0, 1, 3)]
        own = [(far + patch, 0, PATCH, pb_ref[0, head] * log2e), (block[2], 0, PATCH, adds[2])]
        return own + [(block[slot], 0, count, adds[slot]) for slot in (0, 1, 3)]

    inside = [event for event in late if event[1] in (relay_step, forward_step)][:2]
    after = [event for event in late if event not in inside]

    def early_pair(step, carry):
        for turn, (_, act, args) in zip((2, 4), inside):

            @pl.when(step == turn)
            def _():
                act(*args)

        def finish(slot, patch, parity, before, top, total, mixed):
            top_ref[slot] = top
            total_ref[slot] = total
            mixed_ref[slot] = mixed

        attend(step, patches, False, parts_of, q_ref, k_ref, vt_ref, top_ref, finish)
        return carry

    lax.fori_loop(0, pairs, early_pair, 0)
    for _, act, args in after:
        act(*args)

    share = features // cycle
    grain = gsend_ref.shape[1]
    per_pair = LANES // grain
    per_owner = share // grain

    def pair_copy(index):
        slot = lax.div(index, 2 * per_owner) * per_owner + lax.rem(index, per_owner)
        return slot, remote(gsend_ref.at[index], gpair_ref.at[slot], pair_send.at[slot], pair_recv.at[slot],
                            {"space": partner})

    def share_copy(slot):
        owner = lax.div(slot, per_owner)
        gap = lax.rem(chip - owner + chips, chips)
        there = jnp.maximum(gap - 1, 0) * per_owner + lax.rem(slot, per_owner)
        return owner, remote(gsum_ref.at[slot], grecv_ref.at[there], share_send.at[slot], share_recv.at[there],
                             {"space": owner * 2 + core})

    def gather_pair(step):
        for part in range(per_pair):
            index = step * per_pair + part

            @pl.when(lax.rem(lax.div(index, per_owner), 2) == core)
            def _():
                slot, copy = pair_copy(index)
                copy.wait_recv()
                both = gsend_ref[index].astype(jnp.float32) + gpair_ref[slot].astype(jnp.float32)
                gsum_ref[slot] = both.astype(jnp.bfloat16)
                owner, copy = share_copy(slot)

                @pl.when(owner != chip)
                def _():
                    copy.start()

    def step_of(turn):
        return lax.rem(lax.div(chip * pairs, chips) + 2 + turn, pairs)

    def pair(turn, carry):
        step = step_of(turn)

        def finish(slot, patch, parity, before, top, total, mixed):
            fade = jnp.exp2(before - top)
            mixed = (mixed + mixed_ref[slot] * fade) * (1.0 / (total + total_ref[slot] * fade))
            rows = pl.ds(pl.multiple_of(step * LANES + parity * HD, HD), HD)
            attn_ref[rows, patch * PATCH : (patch + 1) * PATCH] = mixed.astype(jnp.bfloat16)

        attend(step, patches, True, parts_of, q_ref, k_ref, vt_ref, top_ref, finish)
        rows = pl.ds(pl.multiple_of(step * LANES, LANES), LANES)
        total = jnp.dot(attn_ref[rows, :], cot_ref[...], preferred_element_type=jnp.float32).astype(jnp.bfloat16)
        for part in range(per_pair):
            gsend_ref[step * per_pair + part] = total[part * grain : (part + 1) * grain]
        for part in range(per_pair):
            index = step * per_pair + part

            @pl.when(lax.rem(lax.div(index, per_owner), 2) != core)
            def _():
                pair_copy(index)[1].start()

        @pl.when(turn > 0)
        def _():
            gather_pair(step_of(turn - 1))

        return carry

    lax.fori_loop(0, pairs, pair, 0)
    gather_pair(step_of(pairs - 1))
    mixture = lax.dot_general(
        attn_ref[...], weight_ref[7], (((0,), (0,)), ((), ())), preferred_element_type=jnp.float32
    )
    out_ref[...] = (hid_ref[...].reshape(patches * PATCH, features).astype(jnp.float32) + mixture).astype(jnp.bfloat16)
    sums = []
    for part in range(per_owner):
        sums.append(gsum_ref[chip * per_owner + part].astype(jnp.float32))
        for k in range(chips - 1):
            slot = k * per_owner + part
            remote(gsum_ref.at[0], grecv_ref.at[slot], share_send.at[0], share_recv.at[slot],
                   {"space": partner}).wait_recv()
            sums[-1] = sums[-1] + grecv_ref[slot].astype(jnp.float32)
    gathered = jnp.concatenate(sums, axis=0)
    piece = share // levels
    for i in range(levels):
        lsend_ref[i] = gathered[i * piece : (i + 1) * piece].astype(jnp.bfloat16)
    parts = []
    for k, peer in enumerate(peers):
        parts.append(remote(lsend_ref.at[peer], lrecv_ref.at[k], part_send.at[k], part_recv.at[k], {"level": peer}))
        parts[-1].start()
    gathered = lsend_ref[level].astype(jnp.float32)
    for k, step in enumerate(parts):
        step.wait_recv()
        gathered = gathered + lrecv_ref[k].astype(jnp.float32)
    final_ref[level] = gathered.astype(jnp.bfloat16)
    fulls = []
    for k, peer in enumerate(peers):
        fulls.append(remote(final_ref.at[level], final_ref.at[level], full_send.at[k], full_recv.at[k],
                            {"level": peer}))
        fulls[-1].start()
    for step in fulls:
        step.wait_recv()
    for i in range(levels):
        grad_ref[i * piece : (i + 1) * piece, :] = final_ref[i].astype(jnp.float32)
    for steps in inward + back + [[make() for make in sent], parts, fulls]:
        for step in steps:
            step.wait_send()

    def drained(slot, carry):
        index = lax.div(slot, per_owner) * 2 * per_owner + (1 - core) * per_owner + lax.rem(slot, per_owner)
        pair_copy(index)[1].wait_send()
        owner, copy = share_copy(slot)

        @pl.when(owner != chip)
        def _():
            copy.wait_send()

        return carry

    lax.fori_loop(0, chips * per_owner, drained, 0)


def body(fields, norm_vert, query_vert, keys_vert, values_vert, out_vert, level_bias, norm_patch, query_patch,
         keys_patch, values_patch, out_patch, patch_bias, neighbours, counts, cotangent):
    _, tokens, features = fields.shape
    levels = lax.axis_size("level")
    cycle = lax.axis_size("space")
    patches = tokens // PATCH
    columns = ROWS
    size = levels * columns
    chunks = tokens // size
    pairs = features // LANES
    grain = math.gcd(features // cycle, LANES)
    share = features // cycle
    x = fields.reshape(chunks, levels, columns, features)
    vmem = pl.BlockSpec(memory_space=pltpu.VMEM)
    smem = pl.BlockSpec(memory_space=pltpu.SMEM)
    hbm = pl.BlockSpec(memory_space=pl.ANY)
    narrow = lambda *shape: pltpu.VMEM(shape, jnp.bfloat16)
    dma = lambda *shape: pltpu.SemaphoreType.DMA(shape)
    blocks = 5 * patches
    out, grad = pl.pallas_call(
        functools.partial(whole_kernel, cycle, levels),
        out_shape=(
            jax.ShapeDtypeStruct((tokens, features), jnp.bfloat16),
            jax.ShapeDtypeStruct((share, features), jnp.float32),
        ),
        in_specs=[vmem] * 3 + [hbm] * 9 + [smem] * 4,
        out_specs=(vmem, vmem),
        scratch_shapes=[
            narrow(8, features, features),
            narrow(features, features),
            narrow(features, LANES),
            narrow(LANES, features),
            narrow(tokens, features),
            narrow(chunks, levels, columns, features),
            narrow(chunks, levels, columns, features),
            narrow(chunks, levels, columns, features),
            narrow(chunks, size, features),
            narrow(4, chunks, size, features),
            narrow(tokens, features),
            narrow(blocks, PATCH, features),
            narrow(blocks, features, PATCH),
            narrow(features, tokens),
            narrow(features // grain, grain, features),
            narrow(features // grain // 2, grain, features),
            narrow(features // grain // 2, grain, features),
            narrow((cycle // 2 - 1) * share // grain, grain, features),
            narrow(levels, share // levels, features),
            narrow(levels - 1, share // levels, features),
            narrow(levels, share // levels, features),
            pltpu.VMEM((patches * pairs * 2, 1, PATCH), jnp.float32),
            pltpu.VMEM((patches * pairs * 2, 1, PATCH), jnp.float32),
            pltpu.VMEM((patches * pairs * 2, HD, PATCH), jnp.float32),
            dma(9),
            dma(chunks, levels - 1),
            dma(chunks, levels - 1),
            dma(chunks, levels - 1),
            dma(chunks, levels - 1),
            dma(chunks, 4),
            dma(chunks, 4),
            dma(features // grain // 2),
            dma(features // grain // 2),
            dma(features // grain // 2),
            dma((cycle // 2 - 1) * share // grain),
            dma(levels - 1),
            dma(levels - 1),
            dma(levels - 1),
            dma(levels - 1),
        ],
        compiler_params=pltpu.CompilerParams(
            collective_id=0, has_side_effects=True, vmem_limit_bytes=VMEM_LIMIT
        ),
        name="whole_block",
    )(x, norm_vert, norm_patch, query_vert, keys_vert, values_vert, out_vert, query_patch, keys_patch,
      values_patch, out_patch, cotangent[0], jnp.transpose(level_bias, (1, 2, 0)), patch_bias.T, neighbours, counts)
    return (out[None], grad)


def solution(mesh):
    split = P("level", "space", None)
    return jax.shard_map(
        body,
        mesh=mesh,
        in_specs=(split,) + (P(),) * 12 + (P("space", None), P("space"), split),
        out_specs=(split, P("space", None)),
        check_vma=False,
    )
```

time: 94.8 us -> 92.1 us (0.972)
  Pallas kernels: 91.2 us -> 88.4 us
    pallas_call x1, Pallas kernels: 91.2 us -> 88.4 us  [body(): pl.pallas_call(functools.partial(whole_kernel, cycle, levels), out_shape=...]
where the time goes in v1:
time: 92.1 us; the launch traced here: 91.9 us
  Pallas kernels  88.4 us (96%)
  local copies, waits for them, and re-layouts  2.83 us (3%)
    pallas_call x1, Pallas kernels, body(): pl.pallas_call(functools.partial(whole_kernel, cycle, levels), out_shape=...  88.4 us
    unnamed x4, local copies, waits for them, and re-layouts  2.83 us

profile of v1, /device:TPU:0, one launch (start us, length us, event | category | flops | bytes accessed | tf_op | source)
XLA Modules:
  0.0 91.9 jit_solution(15853313021528172625)
XLA Ops:
  0.6 88.4 %whole_block.1 = (bf16[512,768]{1,0:T(8,128)(2,1)}, f32[96,768]{1,0:T(8,128)}) custom-call(bf16[8,4,16,768]{3,2,1,0:T(8,128)(2,1)} %bitcast.5, f32[768]{0:T(1024)} %nv_ref.1, f32[768]{0:T(1024)} %np_ref.1, bf16[768,768]{1,0:T(8,128)(2,1)} %wqv_hbm.1, bf16[768,768]{1,0:T(8,128)(2,1)} %wkv_hbm.1, bf16[768,768]{1,0:T(8,128)(2,1)} %wvv_hbm.1, ...), custom_call_target="tpu_custom_call" | custom-call | tf_op jit(solution)/shard_map/whole_block/pallas_call | solution.py:467
  89.1 0.0 copy-start
  89.1 2.1 %copy.20 = bf16[1,512,768]{2,1,0:T(8,128)(2,1)} copy(bf16[1,512,768]{2,1,0:T(8,128)(2,1)} %bitcast.7) | data formatting | bytes 1572864
  91.2 0.0 copy-done
  91.2 0.7 copy.21
Async XLA Ops:
  89.1 2.1 %copy-start = (f32[96,768]{1,0:T(8,128)S(1)}, f32[96,768]{1,0:T(8,128)}, u32[]{:S(2)}) copy-start(f32[96,768]{1,0:T(8,128)} %get-tuple-element.9) | copy-start | bytes 884740

commit v2 on v1

--- a/solution.py
+++ b/solution.py
@@ -13,6 +13,8 @@
 LANES = 128
 ROWS = 16
 DEPTH = 3
+STRIPS = 2
+WIDE = 2
 VMEM_LIMIT = 58 * 1024 * 1024
 
 epsilon = 1e-06
@@ -97,22 +99,22 @@
     return jnp.dot(values, raised, preferred_element_type=jnp.float32)
 
 
-def attend(step, patches, second, parts_of, q_ref, k_ref, vt_ref, top_ref, finish):
-    heads = [(patch, parity) for patch in range(patches) for parity in range(2)]
-    parts = [parts_of(patch, step * 2 + parity, second) for patch, parity in heads]
-    slots = [patch * top_ref.shape[0] // patches + step * 2 + parity for patch, parity in heads]
+def attend(steps, patches, second, parts_of, q_ref, k_ref, vt_ref, top_ref, finish):
+    heads = [(step, patch, parity) for step in steps for patch in range(patches) for parity in range(2)]
+    parts = [parts_of(patch, step * 2 + parity, second) for step, patch, parity in heads]
+    slots = [patch * top_ref.shape[0] // patches + step * 2 + parity for step, patch, parity in heads]
     befores = [top_ref[slot] if second else None for slot in slots]
     scores, soft = {}, {}
     for turn in range(len(heads) + 2):
         if turn < len(heads):
-            patch, parity = heads[turn]
-            scores[turn] = score(step, patch, parity, parts[turn], q_ref, k_ref)
+            scores[turn] = score(*heads[turn], parts[turn], q_ref, k_ref)
         if 1 <= turn < len(heads) + 1:
             soft[turn - 1] = soften(scores.pop(turn - 1), parts[turn - 1], befores[turn - 1])
         if turn >= 2:
             at = turn - 2
+            step, patch, parity = heads[at]
             top, total, raised = soft.pop(at)
-            finish(slots[at], *heads[at], befores[at], top, total, mix(step, heads[at][1], raised, parts[at], vt_ref))
+            finish(slots[at], patch, parity, befores[at], top, total, mix(step, parity, raised, parts[at], vt_ref))
 
 
 def remote(src, dst, send, recv, device):
@@ -123,7 +125,7 @@
 
 
 def whole_kernel(cycle, levels, x_ref, nv_ref, np_ref, wqv_hbm, wkv_hbm, wvv_hbm, wov_hbm, wqp_hbm, wkp_hbm, wvp_hbm,
-                 wop_hbm, cot_hbm, lb_ref, pb_ref, nb_ref, count_ref, out_ref, grad_ref, weight_ref, wvt_ref, gather_ref,
+                 wop_hbm, cot_hbm, lb_ref, pb_ref, nb_ref, count_ref, out_ref, grad_ref, block_ref, weight_ref, wvt_ref, gather_ref,
                  spread_ref, cot_ref, in_ref, hsend_ref, hid_ref, own_ref, far_ref, q_ref, k_ref, vt_ref, attn_ref,
                  gsend_ref, gpair_ref, gsum_ref, grecv_ref, lsend_ref, lrecv_ref, final_ref, top_ref, total_ref, mixed_ref, load_sem, in_send,
                  in_recv, back_send, back_recv, halo_send, halo_recv, pair_send, pair_recv, share_send, share_recv, part_send, part_recv,
@@ -306,13 +308,14 @@
         own = [(far + patch, 0, PATCH, pb_ref[0, head] * log2e), (block[2], 0, PATCH, adds[2])]
         return own + [(block[slot], 0, count, adds[slot]) for slot in (0, 1, 3)]
 
-    inside = [event for event in late if event[1] in (relay_step, forward_step)][:2]
+    inside = [event for event in late if event[1] in (relay_step, forward_step)][:3]
     after = [event for event in late if event not in inside]
 
-    def early_pair(step, carry):
-        for turn, (_, act, args) in zip((2, 4), inside):
-
-            @pl.when(step == turn)
+    def early_pair(turn, carry):
+        steps = [turn * WIDE + k for k in range(WIDE)]
+        for when, (_, act, args) in zip((1, 2, 2), inside):
+
+            @pl.when(turn == when)
             def _():
                 act(*args)
 
@@ -321,10 +324,10 @@
             total_ref[slot] = total
             mixed_ref[slot] = mixed
 
-        attend(step, patches, False, parts_of, q_ref, k_ref, vt_ref, top_ref, finish)
+        attend(steps, patches, False, parts_of, q_ref, k_ref, vt_ref, top_ref, finish)
         return carry
 
-    lax.fori_loop(0, pairs, early_pair, 0)
+    lax.fori_loop(0, pairs // WIDE, early_pair, 0)
     for _, act, args in after:
         act(*args)
 
@@ -373,7 +376,7 @@
             rows = pl.ds(pl.multiple_of(step * LANES + parity * HD, HD), HD)
             attn_ref[rows, patch * PATCH : (patch + 1) * PATCH] = mixed.astype(jnp.bfloat16)
 
-        attend(step, patches, True, parts_of, q_ref, k_ref, vt_ref, top_ref, finish)
+        attend([step], patches, True, parts_of, q_ref, k_ref, vt_ref, top_ref, finish)
         rows = pl.ds(pl.multiple_of(step * LANES, LANES), LANES)
         total = jnp.dot(attn_ref[rows, :], cot_ref[...], preferred_element_type=jnp.float32).astype(jnp.bfloat16)
         for part in range(per_pair):
@@ -396,7 +399,9 @@
     mixture = lax.dot_general(
         attn_ref[...], weight_ref[7], (((0,), (0,)), ((), ())), preferred_element_type=jnp.float32
     )
-    out_ref[...] = (hid_ref[...].reshape(patches * PATCH, features).astype(jnp.float32) + mixture).astype(jnp.bfloat16)
+    block_ref[...] = (hid_ref[...].reshape(patches * PATCH, features).astype(jnp.float32) + mixture).astype(jnp.bfloat16)
+    write = pltpu.make_async_copy(block_ref, out_ref, load_sem.at[0])
+    write.start()
     sums = []
     for part in range(per_owner):
         sums.append(gsum_ref[chip * per_owner + part].astype(jnp.float32))
@@ -407,27 +412,20 @@
             sums[-1] = sums[-1] + grecv_ref[slot].astype(jnp.float32)
     gathered = jnp.concatenate(sums, axis=0)
     piece = share // levels
-    for i in range(levels):
-        lsend_ref[i] = gathered[i * piece : (i + 1) * piece].astype(jnp.bfloat16)
-    parts = []
-    for k, peer in enumerate(peers):
-        parts.append(remote(lsend_ref.at[peer], lrecv_ref.at[k], part_send.at[k], part_recv.at[k], {"level": peer}))
-        parts[-1].start()
-    gathered = lsend_ref[level].astype(jnp.float32)
-    for k, step in enumerate(parts):
-        step.wait_recv()
-        gathered = gathered + lrecv_ref[k].astype(jnp.float32)
-    final_ref[level] = gathered.astype(jnp.bfloat16)
-    fulls = []
-    for k, peer in enumerate(peers):
-        fulls.append(remote(final_ref.at[level], final_ref.at[level], full_send.at[k], full_recv.at[k],
-                            {"level": peer}))
-        fulls[-1].start()
-    for step in fulls:
-        step.wait_recv()
-    for i in range(levels):
-        grad_ref[i * piece : (i + 1) * piece, :] = final_ref[i].astype(jnp.float32)
-    for steps in inward + back + [[make() for make in sent], parts, fulls]:
+    strips = lsend_ref.shape[0]
+    width = features // strips
+    for strip in range(strips):
+        for i in range(levels):
+            lsend_ref[strip, i] = gathered[
+                i * piece : (i + 1) * piece, strip * width : (strip + 1) * width
+            ].astype(jnp.bfloat16)
+    parts, fulls = [], []
+    for strip in range(strips):
+        for k, peer in enumerate(peers):
+            parts.append(remote(lsend_ref.at[strip, peer], lrecv_ref.at[strip, k], part_send.at[strip, k],
+                                part_recv.at[strip, k], {"level": peer}))
+            parts[-1].start()
+    for steps in inward + back + [[make() for make in sent]]:
         for step in steps:
             step.wait_send()
 
@@ -443,6 +441,27 @@
         return carry
 
     lax.fori_loop(0, chips * per_owner, drained, 0)
+
+    for strip in range(strips):
+        gathered = lsend_ref[strip, level].astype(jnp.float32)
+        for k in range(levels - 1):
+            parts[strip * (levels - 1) + k].wait_recv()
+            gathered = gathered + lrecv_ref[strip, k].astype(jnp.float32)
+        final_ref[strip, level] = gathered.astype(jnp.bfloat16)
+        for k, peer in enumerate(peers):
+            fulls.append(remote(final_ref.at[strip, level], final_ref.at[strip, level], full_send.at[strip, k],
+                                full_recv.at[strip, k], {"level": peer}))
+            fulls[-1].start()
+    for step in fulls:
+        step.wait_recv()
+    for strip in range(strips):
+        for i in range(levels):
+            grad_ref[i * piece : (i + 1) * piece, strip * width : (strip + 1) * width] = final_ref[strip, i].astype(
+                jnp.float32
+            )
+    for step in parts + fulls:
+        step.wait_send()
+    write.wait()
 
 
 def body(fields, norm_vert, query_vert, keys_vert, values_vert, out_vert, level_bias, norm_patch, query_patch,
@@ -471,8 +490,9 @@
             jax.ShapeDtypeStruct((share, features), jnp.float32),
         ),
         in_specs=[vmem] * 3 + [hbm] * 9 + [smem] * 4,
-        out_specs=(vmem, vmem),
+        out_specs=(hbm, vmem),
         scratch_shapes=[
+            narrow(tokens, features),
             narrow(8, features, features),
             narrow(features, features),
             narrow(features, LANES),
@@ -491,9 +511,9 @@
             narrow(features // grain // 2, grain, features),
             narrow(features // grain // 2, grain, features),
             narrow((cycle // 2 - 1) * share // grain, grain, features),
-            narrow(levels, share // levels, features),
-            narrow(levels - 1, share // levels, features),
-            narrow(levels, share // levels, features),
+            narrow(STRIPS, levels, share // levels, features // STRIPS),
+            narrow(STRIPS, levels - 1, share // levels, features // STRIPS),
+            narrow(STRIPS, levels, share // levels, features // STRIPS),
             pltpu.VMEM((patches * pairs * 2, 1, PATCH), jnp.float32),
             pltpu.VMEM((patches * pairs * 2, 1, PATCH), jnp.float32),
             pltpu.VMEM((patches * pairs * 2, HD, PATCH), jnp.float32),
@@ -508,10 +528,10 @@
             dma(features // grain // 2),
             dma(features // grain // 2),
             dma((cycle // 2 - 1) * share // grain),
-            dma(levels - 1),
-            dma(levels - 1),
-            dma(levels - 1),
-            dma(levels - 1),
+            dma(STRIPS, levels - 1),
+            dma(STRIPS, levels - 1),
+            dma(STRIPS, levels - 1),
+            dma(STRIPS, levels - 1),
         ],
         compiler_params=pltpu.CompilerParams(
             collective_id=0, has_side_effects=True, vmem_limit_bytes=VMEM_LIMIT

time: 92.1 us -> 89.1 us (0.967)
  Pallas kernels: 88.4 us -> 85.5 us
    pallas_call x1, Pallas kernels: 88.4 us -> 85.5 us  [body(): pl.pallas_call(functools.partial(whole_kernel, cycle, levels), out_shape=...]
where the time goes in v2:
time: 89.1 us; the launch traced here: 89 us
  Pallas kernels  85.5 us (96%)
  local copies, waits for them, and re-layouts  2.83 us (3%)
    pallas_call x1, Pallas kernels, body(): pl.pallas_call(functools.partial(whole_kernel, cycle, levels), out_shape=...  85.5 us
    unnamed x4, local copies, waits for them, and re-layouts  2.83 us

profile of v2, /device:TPU:0, one launch (start us, length us, event | category | flops | bytes accessed | tf_op | source)
XLA Modules:
  0.0 89.0 jit_solution(3098833299314980351)
XLA Ops:
  0.6 85.5 %whole_block.1 = (bf16[512,768]{1,0:T(8,128)(2,1)}, f32[96,768]{1,0:T(8,128)}) custom-call(bf16[8,4,16,768]{3,2,1,0:T(8,128)(2,1)} %bitcast.5, f32[768]{0:T(1024)} %nv_ref.1, f32[768]{0:T(1024)} %np_ref.1, bf16[768,768]{1,0:T(8,128)(2,1)} %wqv_hbm.1, bf16[768,768]{1,0:T(8,128)(2,1)} %wkv_hbm.1, bf16[768,768]{1,0:T(8,128)(2,1)} %wvv_hbm.1, ...), custom_call_target="tpu_custom_call" | custom-call | tf_op jit(solution)/shard_map/whole_block/pallas_call | solution.py:486
  86.1 0.0 copy-start
  86.2 2.1 %copy.20 = bf16[1,512,768]{2,1,0:T(8,128)(2,1)} copy(bf16[1,512,768]{2,1,0:T(8,128)(2,1)} %bitcast.7) | data formatting | bytes 1572864
  88.3 0.0 copy-done
  88.3 0.7 copy.21
Async XLA Ops:
  86.1 2.1 %copy-start = (f32[96,768]{1,0:T(8,128)S(1)}, f32[96,768]{1,0:T(8,128)}, u32[]{:S(2)}) copy-start(f32[96,768]{1,0:T(8,128)} %get-tuple-element.9) | copy-start | bytes 884740

commit v3 on v2

--- a/solution.py
+++ b/solution.py
@@ -89,14 +89,15 @@
     if before is not None:
         top = jnp.maximum(top, before)
     raised = [jnp.exp2(s + (a - top)) for s, a in pieces]
-    total = functools.reduce(jnp.add, [jnp.sum(r, axis=0, keepdims=True) for r in raised])
-    return top, total, jnp.concatenate([r.astype(jnp.bfloat16) for r in raised], axis=0)
+    return top, jnp.concatenate([r.astype(jnp.bfloat16) for r in raised], axis=0)
 
 
 def mix(step, parity, raised, parts, vt_ref):
     rows = pl.ds(pl.multiple_of(step * LANES + parity * HD, HD), HD)
     values = jnp.concatenate([vt_ref[block, rows, pl.ds(first, count)] for block, first, count, _ in parts], axis=1)
-    return jnp.dot(values, raised, preferred_element_type=jnp.float32)
+    values = jnp.concatenate([values, jnp.ones((ROWS, values.shape[1]), jnp.bfloat16)], axis=0)
+    mixed = jnp.dot(values, raised, preferred_element_type=jnp.float32)
+    return mixed[HD : HD + 1], mixed[:HD]
 
 
 def attend(steps, patches, second, parts_of, q_ref, k_ref, vt_ref, top_ref, finish):
@@ -113,8 +114,8 @@
         if turn >= 2:
             at = turn - 2
             step, patch, parity = heads[at]
-            top, total, raised = soft.pop(at)
-            finish(slots[at], patch, parity, befores[at], top, total, mix(step, parity, raised, parts[at], vt_ref))
+            top, raised = soft.pop(at)
+            finish(slots[at], patch, parity, befores[at], top, *mix(step, parity, raised, parts[at], vt_ref))
 
 
 def remote(src, dst, send, recv, device):

time: 89.1 us -> 88.9 us (level)
  no operation moved by 1% of the time
where the time goes in v3:
time: 88.9 us; the launch traced here: 88.7 us
  Pallas kernels  85.3 us (96%)
  local copies, waits for them, and re-layouts  2.83 us (3%)
    pallas_call x1, Pallas kernels, body(): pl.pallas_call(functools.partial(whole_kernel, cycle, levels), out_shape=...  85.3 us
    unnamed x4, local copies, waits for them, and re-layouts  2.83 us

profile of v3, /device:TPU:0, one launch (start us, length us, event | category | flops | bytes accessed | tf_op | source)
XLA Modules:
  0.0 88.7 jit_solution(1584694425981782266)
XLA Ops:
  0.6 85.3 %whole_block.1 = (bf16[512,768]{1,0:T(8,128)(2,1)}, f32[96,768]{1,0:T(8,128)}) custom-call(bf16[8,4,16,768]{3,2,1,0:T(8,128)(2,1)} %bitcast.5, f32[768]{0:T(1024)} %nv_ref.1, f32[768]{0:T(1024)} %np_ref.1, bf16[768,768]{1,0:T(8,128)(2,1)} %wqv_hbm.1, bf16[768,768]{1,0:T(8,128)(2,1)} %wkv_hbm.1, bf16[768,768]{1,0:T(8,128)(2,1)} %wvv_hbm.1, ...), custom_call_target="tpu_custom_call" | custom-call | tf_op jit(solution)/shard_map/whole_block/pallas_call | solution.py:487
  85.9 0.0 copy-start
  85.9 2.1 %copy.20 = bf16[1,512,768]{2,1,0:T(8,128)(2,1)} copy(bf16[1,512,768]{2,1,0:T(8,128)(2,1)} %bitcast.7) | data formatting | bytes 1572864
  88.0 0.0 copy-done
  88.0 0.7 copy.21
Async XLA Ops:
  85.9 2.1 %copy-start = (f32[96,768]{1,0:T(8,128)S(1)}, f32[96,768]{1,0:T(8,128)}, u32[]{:S(2)}) copy-start(f32[96,768]{1,0:T(8,128)} %get-tuple-element.9) | copy-start | bytes 884740
